TPU v7x, 32 devices: a whole 2x2x4 slice. The times are simulated.
32 devices in a mesh: users: 2 (over x), hist: 8 (over z, y), head: 2 (over core).
Axes of the slice: x: 2, y: 2, z: 4, core: 2. Of those that a mesh axis runs over, the one named last changes fastest.
Arguments:
- candidates: bfloat16 [2048, 512], P(('users', 'hist')), parts along dimension 0, may hold values from -6 to 6
- key_cache: bfloat16 [2, 32768, 512], P(None, ('users', 'hist'), 'head'), parts along dimension 1, may hold values from -6 to 6
- value_cache: bfloat16 [2, 32768, 512], P(None, ('users', 'hist'), 'head'), parts along dimension 1, may hold values from -6 to 6
- w_in: bfloat16 [2, 512, 4, 512], P(None, None, None, 'head'), may hold values from -0.25 to 0.25
- w_out: bfloat16 [2, 512, 512], P(None, 'head'), may hold values from -0.25 to 0.25
- rab_table: float32 [2, 32, 8], P(None, None, 'head'), may hold values from -4 to 4
- hist_len: int32 [16], P(('users', 'hist')), parts along dimension 0, may hold values from 1 to 2048, 8192 in all
- hist_bucket: int32 [32768], P(('users', 'hist')), parts along dimension 0, may hold values from 0 to 31
- visible: int32 [8, 128], P(None, ('users', 'hist')), parts along dimension 1, may hold values 0 or 1
Outputs:
- candidate_out: bfloat16 [2048, 512], P(('users', 'hist')), parts along dimension 0
There are 2 independent parts, one for each index of `users`. A program takes and returns all parts, laid end to end along the dimension named above; an argument that names none is the same for every part. Nothing has to cross between parts.
Inputs may be any that keep to these rules, and one draw needn't show every extreme that they name: `hist_len`: entry s counts the valid events at the start of history shard s; the entries sum to 8192 and the largest is 2048. visible[m, b] is 1 where microbatch m sees history events b * 256 to (b + 1) * 256 - 1.
All inputs are finite; a program needn't handle non-finite values.
Results may differ from a plain program's by a relative error of at most 0.019.
Values may be sent and summed in bfloat16 or wider, within the bound.
No kernel may reach another device: no remote copies, remote signals or barrier semaphores. Data moves between devices by JAX's collectives and lax.ppermute only.
A program may use at most 64 MiB of HBM per device.

v0:
```python
import jax
import jax.numpy as jnp
from jax import lax
from jax.sharding import PartitionSpec as P

D = 512
HEADS = 8
DH = 64
LAYERS = 2
NB = 32
BLOCK = 256
MICRO = 8
C = 1024
epsilon = 1e-05


def shards(
    candidates, key_cache, value_cache, w_in, w_out, rab_table, hist_len, hist_bucket, visible
):
    width = HEADS * DH
    factor = DH ** (-0.5)
    local_len = hist_len[0]
    hist_dev = key_cache.shape[1]
    width_local = key_cache.shape[2]
    heads_local = width_local // DH
    key_block = min(512, hist_dev)
    row_count = candidates.shape[0]
    visible_float = visible.astype(jnp.float32)
    stream = lax.all_gather(candidates, "hist", axis=0, tiled=True).astype(jnp.float32)
    for layer_index in range(LAYERS):
        project_average = jnp.mean(stream, axis=-1, keepdims=True)
        centred = stream - project_average
        variance = jnp.mean(centred * centred, axis=-1, keepdims=True)
        normed = (centred * lax.rsqrt(variance + epsilon)).astype(jnp.bfloat16)
        projected = jnp.dot(
            normed,
            w_in[layer_index].reshape(D, 4 * width_local),
            preferred_element_type=jnp.float32,
        )
        projected = jax.nn.silu(projected).astype(jnp.bfloat16).reshape(-1, 4, width_local)
        queries = projected[:, 0]
        keys_new = projected[:, 1]
        values_new = projected[:, 2]
        gates = projected[:, 3]
        one_hot = (hist_bucket[:, None] == jnp.arange(NB, dtype=jnp.int32)[None, :]).astype(
            jnp.float32
        )
        bias = jnp.dot(one_hot, rab_table[layer_index], precision=lax.Precision.HIGHEST)
        attend_query_count = queries.shape[0]
        micro_ids = jnp.arange(attend_query_count, dtype=jnp.int32) // (C // MICRO)
        picking = (micro_ids[:, None] == jnp.arange(MICRO, dtype=jnp.int32)[None, :]).astype(
            jnp.float32
        )
        visible_rows = jnp.dot(picking, visible_float, precision=lax.Precision.HIGHEST)
        attend_query_heads = queries.reshape(attend_query_count, heads_local, DH)
        cached_keys = key_cache[layer_index]
        cached_values = value_cache[layer_index]

        def block_step(block_index, summed):
            key_start = block_index * key_block

            def compute(held):
                key_part = lax.dynamic_slice_in_dim(cached_keys, key_start, key_block, 0).reshape(
                    key_block, heads_local, DH
                )
                value_part = lax.dynamic_slice_in_dim(
                    cached_values, key_start, key_block, 0
                ).reshape(key_block, heads_local, DH)
                bias_part = lax.dynamic_slice_in_dim(bias, key_start, key_block, 0)
                visible_part = lax.dynamic_slice_in_dim(
                    visible_rows, key_start // BLOCK, key_block // BLOCK, 1
                )
                positions = key_start + jnp.arange(key_block, dtype=jnp.int32)
                valid = (positions < local_len).astype(jnp.float32)
                masking = (
                    jnp.repeat(visible_part, BLOCK, axis=1, total_repeat_length=key_block)
                    * valid[None, :]
                )
                scores = jnp.einsum(
                    "rhd,khd->hrk", attend_query_heads, key_part, preferred_element_type=jnp.float32
                )
                scores = scores * factor + bias_part.T[:, None, :]
                weights = (jax.nn.silu(scores) * masking[None]).astype(jnp.bfloat16)
                return held + jnp.einsum(
                    "hrk,khd->rhd", weights, value_part, preferred_element_type=jnp.float32
                )

            return lax.cond(key_start < local_len, compute, lambda held: held, summed)

        summed = lax.fori_loop(
            0,
            hist_dev // key_block,
            block_step,
            jnp.zeros((attend_query_count, heads_local, DH), jnp.float32),
        )
        terms = summed.reshape(attend_query_count, width_local)
        attended = lax.psum(terms.astype(jnp.bfloat16), "hist").astype(jnp.float32)
        finish_attended = attended
        query_count = finish_attended.shape[0]
        query_heads = queries.astype(jnp.float32).reshape(query_count, heads_local, DH)
        key_heads = keys_new.astype(jnp.float32).reshape(query_count, heads_local, DH)
        value_heads = values_new.astype(jnp.float32).reshape(query_count, heads_local, DH)
        own_score = jax.nn.silu(jnp.sum(query_heads * key_heads, axis=-1) * factor)
        finish_attended = finish_attended + (own_score[..., None] * value_heads).reshape(
            query_count, width_local
        )
        totals = lax.psum(
            (
                jnp.sum(finish_attended, axis=-1),
                jnp.sum(finish_attended * finish_attended, axis=-1),
            ),
            "head",
        )
        average = (totals[0] / width)[:, None]
        squares = (totals[1] / width)[:, None]
        normalized = (finish_attended - average) * lax.rsqrt(squares - average * average + epsilon)
        gated = (normalized * gates.astype(jnp.float32)).astype(jnp.bfloat16)
        update = lax.psum(
            jnp.dot(gated, w_out[layer_index], preferred_element_type=jnp.float32).astype(
                jnp.bfloat16
            ),
            "head",
        ).astype(jnp.float32)
        stream = stream + update
    own_start = lax.axis_index("hist") * row_count
    return lax.dynamic_slice_in_dim(stream, own_start, row_count, 0).astype(jnp.bfloat16)


def solution(mesh):
    placed = (
        P(("users", "hist"), None),
        P(None, ("users", "hist"), "head"),
        P(None, ("users", "hist"), "head"),
        P(None, None, None, "head"),
        P(None, "head", None),
        P(None, None, "head"),
        P(("users", "hist")),
        P(("users", "hist")),
        P(None, ("users", "hist")),
    )
    return jax.shard_map(
        shards, mesh=mesh, in_specs=placed, out_specs=P(("users", "hist"), None), check_vma=False
    )
```

profile of v0, /device:TPU:0, one launch (start us, length us, event | category | flops | bytes accessed | tf_op | source)
XLA Modules:
  0.0 378.6 jit_solution(7019134319419471442)
XLA Ops:
  7.3 3.3 fusion.74
  13.6 1.5 copy.18
  16.8 1.5 copy.19
  19.4 33.2 %all-gather.2.cloned.1.call-done = bf16[1024,512]{1,0:T(8,128)(2,1)} async-done(((bf16[128,512]{1,0:T(8,128)(2,1)}), bf16[1024,512]{1,0:T(8,128)(2,1)}) %all-gather.2.cloned.1.call-update) | async-done | bytes 1048592 | tf_op jit(solution)/shard_map/all_gather | solution.py:29
  52.6 1.5 convert_reduce_fusion
  54.1 1.7 fusion.38
  55.9 2.6 multiply_convert_fusion.1
  62.0 15.1 %while.34 = (s32[]{:T(128)}, f32[1024,4,64]{0,2,1:T(8,128)}, s32[]{:T(128)}, bf16[2048,256]{0,1:T(8,128)(2,1)}, bf16[2048,256]{0,1:T(8,128)(2,1)}, /*index=5*/bf...) while((s32[]{:T(128)}, f32[1024,4,64]{0,2,1:T(8,128)}, ...), condition=%wide.region_5.7_spmd, body=%wide.region_2.6_spmd.sunk | while | flops 554437120 | bytes 14733740 | solution.py:90
  62.6 12.4 %conditional.4 = (f32[1024,4,64]{0,2,1:T(8,128)}) conditional(s32[]{:T(128)} %convert_element_type.273, f32[1024,4,64]{0,2,1:T(8,128)} %get-tuple-element.543, (s32[]{:T(128)}, bf16[2048,256]{0,1:T(8,128)(2,1)}, bf16[2048,256]{0,1:T(8,128)(2,1)}, bf16[1024,4,64]{0,2,1:T(8,128)(2,1)}, f32[2048,4]{0,1:T(4,128)S(1)}, /*index=5*/f32[1024,8]{0,1:T(8,128)S(1)}, ...), branch_computations={%region_3.3_spmd, %region_4.5_spmd} | conditional | flops 554437120 | bytes 14733549 | solution.py:88
  63.4 1.8 gather_fusion
  65.9 1.5 bitcast_multiply_fusion.1
  68.5 6.6 %fusion.12 = f32[1024,4,64]{0,2,1:T(8,128)} fusion(f32[1024,4,64]{0,2,1:T(8,128)} %get-tuple-element.336, bf16[512,4,64]{0,2,1:T(8,128)(2,1)S(1)} %bitcast.148, f32[1024,512]{0,1:T(8,128)} %bitcast_multiply_fusion.1, f32[4,512]{1,0:T(4,128)S(1)} %dynamic-slice_bitcast_fusion, bf16[512,4,64]{0,2,1:T(8,128)(2,1)S(1)} %bitcast.147, ...), kind=kOutput, calls=%fused_computation.13 | convolution fusion | flops 553910272 | bytes 5251072 | tf_op jit(solution)/shard_map/while/body/eval_jaxpr/cond/branch_1_fun/hrk,khd->rhd/dot_general | solution.py:84
  77.1 2.2 convert_element_type.165
  79.6 108.4 %all-reduce.7.cloned.1.call-done = bf16[1024,256]{0,1:T(8,128)(2,1)} async-done(((bf16[1024,256]{0,1:T(8,128)(2,1)}), bf16[1024,256]{0,1:T(8,128)(2,1)}) %all-reduce.7.cloned.1.call-update) | async-done | bytes 524304 | tf_op jit(solution)/shard_map/psum | solution.py:97
  188.0 1.5 fusion.53
  189.5 2.5 all-reduce.1
  192.0 1.8 fusion.44
  193.8 2.5 convolution_convert_fusion.1
  199.2 1.5 copy.21
  201.4 13.7 %all-reduce.9.cloned.1.call-done = bf16[1024,512]{1,0:T(8,128)(2,1)} async-done(((bf16[1024,512]{1,0:T(8,128)(2,1)}), bf16[1024,512]{1,0:T(8,128)(2,1)}) %all-reduce.9.cloned.1.call-update) | async-done | bytes 1048592 | tf_op jit(solution)/shard_map/psum | solution.py:118
  215.1 1.7 fusion.72
  216.8 1.8 multiply_reduce_fusion
  218.6 2.6 multiply_convert_fusion
  223.1 14.0 %while.35 = (s32[]{:T(128)}, f32[1024,4,64]{0,2,1:T(8,128)S(1)}, s32[]{:T(128)}, bf16[2048,256]{0,1:T(8,128)(2,1)}, bf16[2048,256]{0,1:T(8,128)(2,1)}, /*index=5...) while((s32[]{:T(128)}, f32[1024,4,64]{0,2,1:T(8,128)S(1)}, ...), condition=%wide.region_18.20_spmd, body=%wide.region_15.19_spmd.sunk | while | flops 554437120 | bytes 14733740 | solution.py:90
  223.8 11.3 %conditional.5 = (f32[1024,4,64]{0,2,1:T(8,128)S(1)}) conditional(s32[]{:T(128)} %convert_element_type.274, f32[1024,4,64]{0,2,1:T(8,128)S(1)} %get-tuple-element.573, (s32[]{:T(128)}, bf16[2048,256]{0,1:T(8,128)(2,1)}, bf16[2048,256]{0,1:T(8,128)(2,1)}, bf16[1024,4,64]{0,2,1:T(8,128)(2,1)}, f32[2048,4]{0,1:T(4,128)S(1)}, ...), branch_computations={%region_16.17_spmd, %region_17.18_spmd} | conditional | flops 554437120 | bytes 14733549 | solution.py:88
  224.5 1.8 gather_fusion.1
  227.0 1.5 bitcast_multiply_fusion.3
  229.6 5.4 %fusion.30 = f32[1024,4,64]{0,2,1:T(8,128)S(1)} fusion(f32[1024,4,64]{0,2,1:T(8,128)S(1)} %get-tuple-element.353, bf16[512,4,64]{0,2,1:T(8,128)(2,1)S(1)} %bitcast.150, f32[1024,512]{0,1:T(8,128)} %bitcast_multiply_fusion.3, f32[4,512]{1,0:T(4,128)S(1)} %dynamic-slice_bitcast_fusion.1, bf16[512,4,64]{0,2,1:T(8,128)(2,1)S(1)} %bitcast.149, ...), kind=kOutput, calls=%fused_computation.34 | convolution fusion | flops 553910272 | bytes 5251072 | tf_op jit(solution)/shard_map/while/body/eval_jaxpr/cond/branch_1_fun/hrk,khd->rhd/dot_general | solution.py:84
  239.6 105.4 %all-reduce.11.cloned.1.call-done = bf16[1024,256]{0,1:T(8,128)(2,1)} async-done(((bf16[1024,256]{0,1:T(8,128)(2,1)}), bf16[1024,256]{0,1:T(8,128)(2,1)}) %all-reduce.11.cloned.1.call-update) | async-done | bytes 524304 | tf_op jit(solution)/shard_map/psum | solution.py:97
  346.3 2.5 all-reduce
  351.6 18.7 %all-reduce.13.cloned.1.call-done = bf16[1024,512]{1,0:T(8,128)(2,1)} async-done(((bf16[1024,512]{1,0:T(8,128)(2,1)}), bf16[1024,512]{1,0:T(8,128)(2,1)}) %all-reduce.13.cloned.1.call-update) | async-done | bytes 1048592 | tf_op jit(solution)/shard_map/psum | solution.py:118
  370.4 1.7 fusion.58
  (89 shorter events, 27.4 us)
Async XLA Ops:
  6.5 46.1 %all-gather.2.cloned.1.call-start = ((), (), s32[]{:S(2)}) async-start(), calls=%async_computation | async-start | bytes 1179648 | tf_op jit(solution)/shard_map/all_gather | solution.py:29
  7.3 180.8 %all-reduce.7.cloned.1.call-start = ((), (), s32[]{:S(2)}) async-start(), calls=%async_computation.1 | async-start | bytes 1048576 | tf_op jit(solution)/shard_map/psum | solution.py:97
  10.6 2.0 copy-start.8
  13.6 2.0 copy-start.9
  16.7 1.5 copy-start.16
  16.8 1.9 copy-start.15
  16.8 2.0 copy-start.17
  16.8 39.1 %copy-start.12 = (bf16[64,8,4,256]{3,1,2,0:T(8,128)(2,1)S(1)}, bf16[64,8,4,256]{3,1,2,0:T(8,128)(2,1)}, u32[]{:S(2)}) copy-start(bf16[64,8,4,256]{3,1,2,0:T(8,128)(2,1)} %copy.22) | copy-start | bytes 3145732
  52.6 3.3 copy-start
  58.5 1.3 copy-start.7
  77.1 2.3 copy-start.10
  77.1 2.3 copy-start.11
  79.3 135.8 %all-reduce.9.cloned.1.call-start = ((), (), s32[]{:S(2)}) async-start(), calls=%async_computation.2 | async-start | bytes 2097152 | tf_op jit(solution)/shard_map/psum | solution.py:118
  192.0 4.6 %copy-start.1 = (bf16[1,512,4,256]{3,2,1,0:T(4,128)(2,1)S(1)}, bf16[1,512,4,256]{3,2,1,0:T(4,128)(2,1)}, u32[]{:S(2)}) copy-start(bf16[1,512,4,256]{3,2,1,0:T(4,128)(2,1)} %get-tuple-element.422) | copy-start | bytes 3145732
  193.8 4.0 %copy-start.2 = (bf16[1,2048,256]{2,1,0:T(8,128)(2,1)S(1)}, bf16[1,2048,256]{2,1,0:T(8,128)(2,1)}, u32[]{:S(2)}) copy-start(bf16[1,2048,256]{2,1,0:T(8,128)(2,1)} %get-tuple-element.426) | copy-start | bytes 3145732
  196.3 148.6 %all-reduce.11.cloned.1.call-start = ((), (), s32[]{:S(2)}) async-start(), calls=%async_computation.3 | async-start | bytes 1048576 | tf_op jit(solution)/shard_map/psum | solution.py:97
  197.8 1.4 copy-start.3
  215.1 1.7 copy-start.4
  216.8 1.9 copy-start.13
  221.3 1.7 copy-start.5
  237.1 107.8 %copy-start.6 = (bf16[1024,1024]{0,1:T(8,128)(2,1)S(1)}, bf16[1024,1024]{0,1:T(8,128)(2,1)}, u32[]{:S(2)}) copy-start(bf16[1024,1024]{0,1:T(8,128)(2,1)} %copy-done.5) | copy-start | bytes 6291460
  238.0 132.3 %all-reduce.13.cloned.1.call-start = ((), (), s32[]{:S(2)}) async-start(), calls=%async_computation.4 | async-start | bytes 2097152 | tf_op jit(solution)/shard_map/psum | solution.py:118
  238.1 112.0 %copy-start.14 = (bf16[2,256,512]{2,1,0:T(8,128)(2,1)S(1)}, bf16[2,256,512]{2,1,0:T(8,128)(2,1)}, u32[]{:S(2)}) copy-start(bf16[2,256,512]{2,1,0:T(8,128)(2,1)} %param.27) | copy-start | bytes 1572868
Sparse Core Ops, SparseCore 0:
  9.5 43.0 all-gather.1
  79.4 108.5 all-reduce.6
  196.5 18.5 all-reduce.8
  238.2 106.7 all-reduce.10
  351.7 18.5 all-reduce.12
where the time goes:
time: 380 us; the launch traced here: 379 us
  waiting for transfers between devices  280 us (74%)
  local copies, waits for them, and re-layouts  26.2 us (7%)
  other arithmetic  24.7 us (6%)
  matrix products  23.1 us (6%)
  between operations  13.4 us (4%)
  loops' own time  5.58 us (1%)
  blocking collectives  4.99 us (1%)
    psum x2, waiting for transfers between devices, shards(): attended = lax.psum(terms.astype(jnp.bfloat16), 'hist').astype(jnp.float32)  214 us
    all_gather x1, waiting for transfers between devices, shards(): lax.all_gather(candidates, 'hist', axis=0, tiled=True).astype(jnp.float32)  33.2 us
    psum x2, waiting for transfers between devices, shards(): lax.psum(jnp.dot(gated, w_out[layer_index], preferred_element_type=jnp.fl...  32.4 us
    dot_general x2, matrix products, compute(): jnp.einsum('hrk,khd->rhd', weights, value_part, preferred_element_type=jn...  12 us
    unnamed x42, local copies, waits for them, and re-layouts  11.4 us
  transfers between devices with their start and end apart: 5, of which 5 were waited for; matrix products, arithmetic and copies ran while one was open for 5% of the time, Pallas kernels for 0%

commit v1 on v0

--- a/solution.py
+++ b/solution.py
@@ -2,6 +2,7 @@
 import jax.numpy as jnp
 from jax import lax
 from jax.sharding import PartitionSpec as P
+from jax.lax import all_gather
 
 D = 512
 HEADS = 8
@@ -115,12 +116,16 @@
         squares = (totals[1] / width)[:, None]
         normalized = (finish_attended - average) * lax.rsqrt(squares - average * average + epsilon)
         gated = (normalized * gates.astype(jnp.float32)).astype(jnp.bfloat16)
-        update = lax.psum(
-            jnp.dot(gated, w_out[layer_index], preferred_element_type=jnp.float32).astype(
-                jnp.bfloat16
-            ),
-            "head",
-        ).astype(jnp.float32)
+        update = (
+            all_gather(
+                jnp.dot(gated, w_out[layer_index], preferred_element_type=jnp.float32).astype(
+                    jnp.bfloat16
+                ),
+                "head",
+            )
+            .sum(axis=0)
+            .astype(jnp.float32)
+        )
         stream = stream + update
     own_start = lax.axis_index("hist") * row_count
     return lax.dynamic_slice_in_dim(stream, own_start, row_count, 0).astype(jnp.bfloat16)

time: 380 us -> 366 us (0.963)
  waiting for transfers between devices: 280 us -> 262 us
  other arithmetic: 24.7 us -> 28.6 us
    psum x2 -> x0, waiting for transfers between devices: 32.4 us -> none  [shards(): lax.psum(jnp.dot(gated, w_out[layer_index], preferred_element_type=jnp.fl...]
    all_gather x0 -> x2, waiting for transfers between devices: none -> 14.8 us  [shards(): all_gather(jnp.dot(gated, w_out[layer_index], preferred_element_type=jnp....]
    reduce_sum x0 -> x2, other arithmetic: none -> 5.23 us  [shards(): update = all_gather(jnp.dot(gated, w_out[layer_index], preferred_element_...]
    unnamed x42 -> x40, local copies, waits for them, and re-layouts: 11.4 us -> 11.4 us
where the time goes in v1:
time: 366 us; the launch traced here: 365 us
  waiting for transfers between devices  262 us (72%)
  other arithmetic  28.6 us (8%)
  local copies, waits for them, and re-layouts  26.2 us (7%)
  matrix products  23.1 us (6%)
  between operations  13.4 us (4%)
  loops' own time  5.58 us (2%)
  blocking collectives  4.99 us (1%)
    psum x2, waiting for transfers between devices, shards(): attended = lax.psum(terms.astype(jnp.bfloat16), 'hist').astype(jnp.float32)  214 us
    all_gather x1, waiting for transfers between devices, shards(): lax.all_gather(candidates, 'hist', axis=0, tiled=True).astype(jnp.float32)  33 us
    all_gather x2, waiting for transfers between devices, shards(): all_gather(jnp.dot(gated, w_out[layer_index], preferred_element_type=jnp....  14.8 us
    dot_general x2, matrix products, compute(): jnp.einsum('hrk,khd->rhd', weights, value_part, preferred_element_type=jn...  12 us
    unnamed x40, local copies, waits for them, and re-layouts  11.4 us
  transfers between devices with their start and end apart: 5, of which 5 were waited for; matrix products, arithmetic and copies ran while one was open for 5% of the time, Pallas kernels for 0%

profile of v1, /device:TPU:0, one launch (start us, length us, event | category | flops | bytes accessed | tf_op | source)
XLA Modules:
  0.0 364.6 jit_solution(7991527446865642305)
XLA Ops:
  7.3 3.3 fusion.74
  16.8 1.5 copy.19
  19.4 33.0 %all-gather.6.cloned.1.call-done = bf16[1024,512]{1,0:T(8,128)(2,1)} async-done(((bf16[128,512]{1,0:T(8,128)(2,1)}), bf16[1024,512]{1,0:T(8,128)(2,1)}) %all-gather.6.cloned.1.call-update) | async-done | bytes 1048592 | tf_op jit(solution)/shard_map/all_gather | solution.py:30
  52.5 1.5 convert_reduce_fusion
  54.0 1.7 fusion.38
  55.8 2.6 multiply_convert_fusion.1
  61.9 15.1 %while.34 = (s32[]{:T(128)}, f32[1024,4,64]{0,2,1:T(8,128)}, s32[]{:T(128)}, bf16[2048,256]{0,1:T(8,128)(2,1)}, bf16[2048,256]{0,1:T(8,128)(2,1)}, /*index=5*/bf...) while((s32[]{:T(128)}, f32[1024,4,64]{0,2,1:T(8,128)}, ...), condition=%wide.region_5.7_spmd, body=%wide.region_2.6_spmd.sunk | while | flops 554437120 | bytes 14733740 | solution.py:91
  62.5 12.4 %conditional.4 = (f32[1024,4,64]{0,2,1:T(8,128)}) conditional(s32[]{:T(128)} %convert_element_type.277, f32[1024,4,64]{0,2,1:T(8,128)} %get-tuple-element.543, (s32[]{:T(128)}, bf16[2048,256]{0,1:T(8,128)(2,1)}, bf16[2048,256]{0,1:T(8,128)(2,1)}, bf16[1024,4,64]{0,2,1:T(8,128)(2,1)}, f32[2048,4]{0,1:T(4,128)S(1)}, /*index=5*/f32[1024,8]{0,1:T(8,128)S(1)}, ...), branch_computations={%region_3.3_spmd, %region_4.5_spmd} | conditional | flops 554437120 | bytes 14733549 | solution.py:89
  63.3 1.8 gather_fusion
  65.8 1.5 bitcast_multiply_fusion.1
  68.4 6.6 %fusion.12 = f32[1024,4,64]{0,2,1:T(8,128)} fusion(f32[1024,4,64]{0,2,1:T(8,128)} %get-tuple-element.336, bf16[512,4,64]{0,2,1:T(8,128)(2,1)S(1)} %bitcast.150, f32[1024,512]{0,1:T(8,128)} %bitcast_multiply_fusion.1, f32[4,512]{1,0:T(4,128)S(1)} %dynamic-slice_bitcast_fusion, bf16[512,4,64]{0,2,1:T(8,128)(2,1)S(1)} %bitcast.149, ...), kind=kOutput, calls=%fused_computation.13 | convolution fusion | flops 553910272 | bytes 5251072 | tf_op jit(solution)/shard_map/while/body/eval_jaxpr/cond/branch_1_fun/hrk,khd->rhd/dot_general | solution.py:85
  77.0 2.2 convert_element_type.169
  79.5 108.4 %all-reduce.5.cloned.1.call-done = bf16[1024,256]{0,1:T(8,128)(2,1)} async-done(((bf16[1024,256]{0,1:T(8,128)(2,1)}), bf16[1024,256]{0,1:T(8,128)(2,1)}) %all-reduce.5.cloned.1.call-update) | async-done | bytes 524304 | tf_op jit(solution)/shard_map/psum | solution.py:98
  187.9 1.5 fusion.53
  189.3 2.5 all-reduce.1
  191.9 1.8 fusion.44
  193.6 2.5 convolution_convert_fusion.1
  201.2 4.9 %all-gather.8.cloned.1.call-done = bf16[2048,512]{1,0:T(8,128)(2,1)} async-done(((bf16[1024,512]{1,0:T(8,128)(2,1)}), bf16[2048,512]{1,0:T(8,128)(2,1)}) %all-gather.8.cloned.1.call-update) | async-done | bytes 2097168 | tf_op jit(solution)/shard_map/all_gather | solution.py:120
  206.1 2.6 reduce_sum.119
  209.0 1.8 multiply_reduce_fusion
  210.8 2.6 multiply_convert_fusion
  215.3 14.0 %while.35 = (s32[]{:T(128)}, f32[1024,4,64]{0,2,1:T(8,128)S(1)}, s32[]{:T(128)}, bf16[2048,256]{0,1:T(8,128)(2,1)}, bf16[2048,256]{0,1:T(8,128)(2,1)}, /*index=5...) while((s32[]{:T(128)}, f32[1024,4,64]{0,2,1:T(8,128)S(1)}, ...), condition=%wide.region_18.20_spmd, body=%wide.region_15.19_spmd.sunk | while | flops 554437120 | bytes 14733740 | solution.py:91
  216.0 11.3 %conditional.5 = (f32[1024,4,64]{0,2,1:T(8,128)S(1)}) conditional(s32[]{:T(128)} %convert_element_type.278, f32[1024,4,64]{0,2,1:T(8,128)S(1)} %get-tuple-element.573, (s32[]{:T(128)}, bf16[2048,256]{0,1:T(8,128)(2,1)}, bf16[2048,256]{0,1:T(8,128)(2,1)}, bf16[1024,4,64]{0,2,1:T(8,128)(2,1)}, f32[2048,4]{0,1:T(4,128)S(1)}, ...), branch_computations={%region_16.17_spmd, %region_17.18_spmd} | conditional | flops 554437120 | bytes 14733549 | solution.py:89
  216.8 1.8 gather_fusion.1
  219.3 1.5 bitcast_multiply_fusion.3
  221.9 5.4 %fusion.30 = f32[1024,4,64]{0,2,1:T(8,128)S(1)} fusion(f32[1024,4,64]{0,2,1:T(8,128)S(1)} %get-tuple-element.353, bf16[512,4,64]{0,2,1:T(8,128)(2,1)S(1)} %bitcast.152, f32[1024,512]{0,1:T(8,128)} %bitcast_multiply_fusion.3, f32[4,512]{1,0:T(4,128)S(1)} %dynamic-slice_bitcast_fusion.1, bf16[512,4,64]{0,2,1:T(8,128)(2,1)S(1)} %bitcast.151, ...), kind=kOutput, calls=%fused_computation.34 | convolution fusion | flops 553910272 | bytes 5251072 | tf_op jit(solution)/shard_map/while/body/eval_jaxpr/cond/branch_1_fun/hrk,khd->rhd/dot_general | solution.py:85
  231.8 105.4 %all-reduce.7.cloned.1.call-done = bf16[1024,256]{0,1:T(8,128)(2,1)} async-done(((bf16[1024,256]{0,1:T(8,128)(2,1)}), bf16[1024,256]{0,1:T(8,128)(2,1)}) %all-reduce.7.cloned.1.call-update) | async-done | bytes 524304 | tf_op jit(solution)/shard_map/psum | solution.py:98
  338.5 2.5 all-reduce
  342.4 1.5 convolution_convert_fusion
  343.9 9.9 %all-gather.10.cloned.1.call-done = bf16[2048,512]{1,0:T(8,128)(2,1)} async-done(((bf16[1024,512]{1,0:T(8,128)(2,1)}), bf16[2048,512]{1,0:T(8,128)(2,1)}) %all-gather.10.cloned.1.call-update) | async-done | bytes 2097168 | tf_op jit(solution)/shard_map/all_gather | solution.py:120
  353.8 2.6 reduce_sum.125
  356.4 1.6 fusion.58
  (89 shorter events, 29.2 us)
Async XLA Ops:
  6.5 46.0 %all-gather.6.cloned.1.call-start = ((), (), s32[]{:S(2)}) async-start(), calls=%async_computation | async-start | bytes 1179648 | tf_op jit(solution)/shard_map/all_gather | solution.py:30
  7.3 180.6 %all-reduce.5.cloned.1.call-start = ((), (), s32[]{:S(2)}) async-start(), calls=%async_computation.1 | async-start | bytes 1048576 | tf_op jit(solution)/shard_map/psum | solution.py:98
  10.6 2.0 copy-start.7
  13.6 2.0 copy-start.8
  16.8 1.5 copy-start.15
  16.8 1.9 copy-start.14
  16.8 2.0 copy-start.16
  16.8 39.0 %copy-start.11 = (bf16[64,8,4,256]{3,1,2,0:T(8,128)(2,1)S(1)}, bf16[64,8,4,256]{3,1,2,0:T(8,128)(2,1)}, u32[]{:S(2)}) copy-start(bf16[64,8,4,256]{3,1,2,0:T(8,128)(2,1)} %copy.22) | copy-start | bytes 3145732
  52.5 3.3 copy-start
  58.4 1.3 copy-start.6
  77.0 2.3 copy-start.9
  77.0 2.3 copy-start.10
  79.2 126.9 %all-gather.8.cloned.1.call-start = ((), (), s32[]{:S(2)}) async-start(), calls=%async_computation.3 | async-start | bytes 3145728 | tf_op jit(solution)/shard_map/all_gather | solution.py:120
  191.9 4.5 %copy-start.1 = (bf16[1,512,4,256]{3,2,1,0:T(4,128)(2,1)S(1)}, bf16[1,512,4,256]{3,2,1,0:T(4,128)(2,1)}, u32[]{:S(2)}) copy-start(bf16[1,512,4,256]{3,2,1,0:T(4,128)(2,1)} %get-tuple-element.422) | copy-start | bytes 3145732
  193.6 4.0 %copy-start.2 = (bf16[1,2048,256]{2,1,0:T(8,128)(2,1)S(1)}, bf16[1,2048,256]{2,1,0:T(8,128)(2,1)}, u32[]{:S(2)}) copy-start(bf16[1,2048,256]{2,1,0:T(8,128)(2,1)} %get-tuple-element.426) | copy-start | bytes 3145732
  196.2 141.1 %all-reduce.7.cloned.1.call-start = ((), (), s32[]{:S(2)}) async-start(), calls=%async_computation.2 | async-start | bytes 1048576 | tf_op jit(solution)/shard_map/psum | solution.py:98
  197.6 1.4 copy-start.3
  209.0 1.8 copy-start.12
  213.5 1.7 copy-start.4
  229.4 107.9 %copy-start.5 = (bf16[1024,1024]{0,1:T(8,128)(2,1)S(1)}, bf16[1024,1024]{0,1:T(8,128)(2,1)}, u32[]{:S(2)}) copy-start(bf16[1024,1024]{0,1:T(8,128)(2,1)} %copy-done.4) | copy-start | bytes 6291460
  230.3 123.5 %all-gather.10.cloned.1.call-start = ((), (), s32[]{:S(2)}) async-start(), calls=%async_computation.4 | async-start | bytes 3145728 | tf_op jit(solution)/shard_map/all_gather | solution.py:120
  230.3 112.1 %copy-start.13 = (bf16[2,256,512]{2,1,0:T(8,128)(2,1)S(1)}, bf16[2,256,512]{2,1,0:T(8,128)(2,1)}, u32[]{:S(2)}) copy-start(bf16[2,256,512]{2,1,0:T(8,128)(2,1)} %param.27) | copy-start | bytes 1572868
Sparse Core Ops, SparseCore 0:
  9.5 42.9 all-gather.5
  79.3 108.5 all-reduce.4
  196.3 9.7 all-gather.7
  230.4 106.7 all-reduce.6
  344.0 9.7 all-gather.9
